TPU v7x, 256 devices: a whole 4x4x8 slice. The times are simulated.
256 devices in a mesh: expert: 64 (over y, z_hi, x, core), hidden: 4 (over z_lo).
Axes of the slice: x: 4, y: 4, z: 8 (z_hi: 2, z_lo: 4; z = z_hi * 4 + z_lo), core: 2. Of those that a mesh axis runs over, the one named last changes fastest.
Arguments:
- tokens: bfloat16 [50176, 768], P(('expert', 'hidden')), may hold values from -512 to 512
- out_grad: bfloat16 [50176, 768], P(('expert', 'hidden')), may hold values from -12 to 12
- slot_router: bfloat16 [768, 256], replicated, may hold values from -0.5 to 0.5
- weight_in: bfloat16 [128, 768, 3072], P('expert', None, 'hidden'), may hold values from -0.21875 to 0.21875
- weight_out: bfloat16 [128, 3072, 768], P('expert', 'hidden'), may hold values from -0.109375 to 0.109375
Outputs:
- token_grad: bfloat16 [50176, 768], P(('expert', 'hidden'))
- router_grad: float32 [768, 256], P('hidden', 'expert')
- weight_in_grad: bfloat16 [128, 768, 3072], P('expert', None, 'hidden')
- weight_out_grad: bfloat16 [128, 3072, 768], P('expert', 'hidden')
All inputs are finite; a program needn't handle non-finite values.
Results may differ from a plain program's by a relative error of at most 0.019.
Values may be sent and summed in bfloat16 or wider, within the bound.
A program may use at most 64 MiB of HBM per device.

v0:
```python
import jax
import jax.numpy as jnp
from jax import lax
from jax.sharding import PartitionSpec as P

D = 768
SLOTS = 2
TOK = 196


def gelu_value(values):
    return 0.5 * values * (1.0 + lax.erf(values * 0.7071067811865476))


def gelu_slope(values):
    return (
        0.5 * (1.0 + lax.erf(values * 0.7071067811865476))
        + values * jnp.exp(-0.5 * values * values) * 0.3989422804014327
    )


def to_experts(stacked_slots):
    crossed = lax.all_to_all(stacked_slots, "expert", split_axis=2, concat_axis=0, tiled=True)
    arrived = lax.all_gather(crossed, "hidden", axis=0, tiled=True)
    return arrived


def to_owners(partials):
    rounded = lax.optimization_barrier(partials.astype(jnp.bfloat16))
    summed = lax.psum_scatter(
        rounded.astype(jnp.float32).astype(jnp.bfloat16), "hidden", scatter_dimension=0, tiled=True
    )
    result = lax.all_to_all(summed, "expert", split_axis=0, concat_axis=2, tiled=True)
    return result


def per_device(tokens, out_grad, slot_router, weight_in, weight_out):
    images = tokens.shape[0] // TOK
    local_experts = weight_in.shape[0]
    inputs = tokens.reshape(images, TOK, D)
    out_grads = out_grad.reshape(images, TOK, D)
    logits = jnp.einsum("btd,dc->btc", inputs, slot_router, preferred_element_type=jnp.float32)
    dispatch = jax.nn.softmax(logits, axis=1)
    combine = jax.nn.softmax(logits, axis=2)
    dispatch16 = dispatch.astype(jnp.bfloat16)
    combine16 = combine.astype(jnp.bfloat16)
    slot_in = jnp.einsum(
        "btc,btd->bcd", dispatch16, inputs, preferred_element_type=jnp.float32
    ).astype(jnp.bfloat16)
    slot_grad = jnp.einsum(
        "btc,btd->bcd", combine16, out_grads, preferred_element_type=jnp.float32
    ).astype(jnp.bfloat16)
    arrived = to_experts(slot_in[:, None])
    received = arrived[:, 0]
    row_count = received.shape[0]
    slot_inputs = received.reshape(row_count, local_experts, SLOTS, D)
    pre_act = jnp.einsum(
        "resd,edf->resf", slot_inputs, weight_in, preferred_element_type=jnp.float32
    )
    activated = gelu_value(pre_act).astype(jnp.bfloat16)
    partial_value = jnp.einsum(
        "resf,efd->resd", activated, weight_out, preferred_element_type=jnp.float32
    )
    slot_inputs, pre_act, activated, forward_part = (
        slot_inputs,
        pre_act,
        activated,
        partial_value.reshape(row_count, 1, local_experts * SLOTS, D),
    )
    slot_out = to_owners(forward_part)[:, 0]
    arrived_grad = to_experts(slot_grad[:, None])
    received_grad = arrived_grad[:, 0]
    row_count = received_grad.shape[0]
    slot_grads = received_grad.reshape(row_count, local_experts, SLOTS, D)
    d_act = jnp.einsum("resd,efd->resf", slot_grads, weight_out, preferred_element_type=jnp.float32)
    d_pre = (d_act * gelu_slope(pre_act)).astype(jnp.bfloat16)
    grad_second = jnp.einsum(
        "resf,resd->efd", activated, slot_grads, preferred_element_type=jnp.float32
    ).astype(jnp.bfloat16)
    grad_first = jnp.einsum(
        "resd,resf->edf", slot_inputs, d_pre, preferred_element_type=jnp.float32
    ).astype(jnp.bfloat16)
    partial_value = jnp.einsum(
        "resf,edf->resd", d_pre, weight_in, preferred_element_type=jnp.float32
    )
    backward_part = partial_value.reshape(row_count, 1, local_experts * SLOTS, D)
    slot_in_grad = to_owners(backward_part)[:, 0]
    d_combine = jnp.einsum("btd,bcd->btc", out_grads, slot_out, preferred_element_type=jnp.float32)
    d_dispatch = jnp.einsum(
        "btd,bcd->btc", inputs, slot_in_grad, preferred_element_type=jnp.float32
    )
    from_combine = combine * (d_combine - jnp.sum(combine * d_combine, axis=2, keepdims=True))
    from_dispatch = dispatch * (d_dispatch - jnp.sum(dispatch * d_dispatch, axis=1, keepdims=True))
    d_logits = (from_combine + from_dispatch).astype(jnp.bfloat16)
    token_grad = (
        jnp.einsum("btc,bcd->btd", dispatch16, slot_in_grad, preferred_element_type=jnp.float32)
        + jnp.einsum("btc,dc->btd", d_logits, slot_router, preferred_element_type=jnp.float32)
    ).astype(jnp.bfloat16)
    router_term = jnp.einsum("btd,btc->dc", inputs, d_logits, preferred_element_type=jnp.float32)
    router_sum = lax.psum(router_term, ("expert", "hidden"))
    row_count = router_term.shape[0] // lax.axis_size("hidden")
    col_count = router_term.shape[1] // lax.axis_size("expert")
    router_grad = lax.dynamic_slice(
        router_sum,
        (lax.axis_index("hidden") * row_count, lax.axis_index("expert") * col_count),
        (row_count, col_count),
    )
    return (token_grad.reshape(images * TOK, D), router_grad, grad_first, grad_second)


def solution(mesh):
    return jax.shard_map(
        per_device,
        mesh=mesh,
        in_specs=(
            P(("expert", "hidden"), None),
            P(("expert", "hidden"), None),
            P(),
            P("expert", None, "hidden"),
            P("expert", "hidden", None),
        ),
        out_specs=(
            P(("expert", "hidden"), None),
            P("hidden", "expert"),
            P("expert", None, "hidden"),
            P("expert", "hidden", None),
        ),
        check_vma=False,
    )
```

profile of v0, /device:TPU:2, one launch (start us, length us, event | category | flops | bytes accessed | tf_op | source)
XLA Modules:
  0.0 541.8 jit_solution(13264223133541740712)
XLA Ops:
  7.2 1.6 fusion.40
  11.4 3.9 reduce.16
  16.5 28.7 %all_to_all.42 = bf16[64,2,1536]{2,1,0:T(2,128)(2,1)} all-to-all(bf16[64,2,1536]{2,1,0:T(2,128)(2,1)S(1)} %reshape.157), channel_id=1, replica_groups=mesh['expert'=64,'hidden'=4] {'expert'}, dimensions={0} | all-to-all | bytes 786432 | tf_op jit(solution)/shard_map/all_to_all | solution.py:23
  45.3 2.7 reshape.158
  48.0 3.0 bitcast_reduce_fusion.1
  51.0 1.8 all_to_all.15
  55.1 3.9 reduce.17
  60.2 26.7 %all_to_all.43 = bf16[64,2,1536]{2,1,0:T(2,128)(2,1)} all-to-all(bf16[64,2,1536]{2,1,0:T(2,128)(2,1)S(1)} %reshape.159), channel_id=1, replica_groups=mesh['expert'=64,'hidden'=4] {'expert'}, dimensions={0} | all-to-all | bytes 786432 | tf_op jit(solution)/shard_map/all_to_all | solution.py:23
  86.9 2.7 reshape.160
  89.7 3.0 bitcast_reduce_fusion
  92.7 1.9 all_to_all.13
  94.8 7.2 %all-gather.5.cloned.1.call-done = bf16[256,1,4,768]{3,2,1,0:T(4,128)(2,1)} async-done(((bf16[64,1,4,768]{3,2,1,0:T(4,128)(2,1)}), bf16[256,1,4,768]{3,2,1,0:T(4,128)(2,1)}) %all-gather.5.cloned.1.call-update) | async-done | bytes 1572880 | tf_op jit(solution)/shard_map/all_gather | solution.py:24
  102.0 1.6 copy.36
  104.8 3.0 fusion.9
  107.8 37.1 %all-gather.3.cloned.1.call-done = bf16[256,1,4,768]{3,2,1,0:T(4,128)(2,1)} async-done(((bf16[64,1,4,768]{3,2,1,0:T(4,128)(2,1)}), bf16[256,1,4,768]{3,2,1,0:T(4,128)(2,1)}) %all-gather.3.cloned.1.call-update) | async-done | bytes 1572880 | tf_op jit(solution)/shard_map/all_gather | solution.py:24
  144.9 1.8 copy.33
  147.1 3.8 fusion.5
  155.0 3.5 fusion.18
  159.8 1.4 copy.60
  161.2 33.9 %reduce-scatter.9.cloned.1.call-done = bf16[64,3072]{1,0:T(8,128)(2,1)} async-done(((bf16[256,3072]{1,0:T(8,128)(2,1)}), bf16[64,3072]{1,0:T(8,128)(2,1)}) %reduce-scatter.9.cloned.1.call-update) | async-done | bytes 393232
  195.1 2.0 reshape.152
  197.1 10.9 %all-to-all-start.2 = ((bf16[64,1,4,768]{3,2,1,0:T(4,128)(2,1)}), bf16[64,1,4,768]{3,2,1,0:T(4,128)(2,1)S(1)}, u32[]{:S(2)}, u32[]{:S(2)}) async-start(bf16[64,1,4,768]{3,2,1,0:T(4,128)(2,1)} %reshape.152), calls=%async_computation.2 | async-start | bytes 786432 | tf_op jit(solution)/shard_map/all_to_all | solution.py:33
  208.0 37.7 %reduce-scatter.11.cloned.1.call-done = bf16[64,3072]{1,0:T(8,128)(2,1)} async-done(((bf16[256,3072]{1,0:T(8,128)(2,1)}), bf16[64,3072]{1,0:T(8,128)(2,1)}) %reduce-scatter.11.cloned.1.call-update) | async-done | bytes 393232
  245.7 2.0 reshape.154
  247.7 11.1 %all-to-all-start.3 = ((bf16[64,1,4,768]{3,2,1,0:T(4,128)(2,1)}), bf16[64,1,4,768]{3,2,1,0:T(4,128)(2,1)}, u32[]{:S(2)}, u32[]{:S(2)}) async-start(bf16[64,1,4,768]{3,2,1,0:T(4,128)(2,1)} %reshape.154), calls=%async_computation.3 | async-start | bytes 786432 | tf_op jit(solution)/shard_map/all_to_all | solution.py:33
  259.2 4.9 bitcast_convert_fusion
  264.1 2.9 bitcast_convert_fusion.1
  268.4 6.4 %all-to-all-done.3 = bf16[64,1,4,768]{3,2,1,0:T(4,128)(2,1)} async-done(((bf16[64,1,4,768]{3,2,1,0:T(4,128)(2,1)}), bf16[64,1,4,768]{3,2,1,0:T(4,128)(2,1)}, u32[]{:S(2)}, u32[]{:S(2)}) %all-to-all-start.3) | async-done | bytes 393248 | tf_op jit(solution)/shard_map/all_to_all | solution.py:33
  274.8 1.8 reshape.146
  276.6 1.5 multiply_reduce_fusion.1
  280.7 2.0 fusion.26
  282.7 251.2 %all-reduce.2.cloned.1.call-done = f32[768,256]{0,1:T(8,128)} async-done(((f32[768,256]{0,1:T(8,128)}), f32[768,256]{0,1:T(8,128)}) %all-reduce.2.cloned.1.call-update) | async-done | bytes 786448 | tf_op jit(solution)/shard_map/psum | solution.py:100
  (49 shorter events, 20.2 us)
Async XLA Ops:
  7.2 97.6 %copy-start = (bf16[2,768,768]{2,1,0:T(8,128)(2,1)S(1)}, bf16[2,768,768]{2,1,0:T(8,128)(2,1)}, u32[]{:S(2)}) copy-start(bf16[2,768,768]{2,1,0:T(8,128)(2,1)} %param.8) | copy-start | bytes 7077892
  7.2 94.8 %all-gather.5.cloned.1.call-start = ((), (), s32[]{:S(2)}) async-start(), calls=%async_computation.7 | async-start | bytes 1966080 | tf_op jit(solution)/shard_map/all_gather | solution.py:24
  52.9 92.0 %all-gather.3.cloned.1.call-start = ((), (), s32[]{:S(2)}) async-start(), calls=%async_computation.6 | async-start | bytes 1966080 | tf_op jit(solution)/shard_map/all_gather | solution.py:24
  94.6 100.5 %reduce-scatter.9.cloned.1.call-start = ((), (), s32[]{:S(2)}) async-start(), calls=%async_computation.9 | async-start | bytes 1966080
  103.6 1.1 copy-start.2
  144.9 2.1 copy-start.7
  146.7 4.1 copy-start.4
  150.8 1.4 copy-start.8
  154.9 90.8 %reduce-scatter.11.cloned.1.call-start = ((), (), s32[]{:S(2)}) async-start(), calls=%async_computation.10 | async-start | bytes 1966080
  197.1 50.6 %all-to-all-start.2 = ((bf16[64,1,4,768]{3,2,1,0:T(4,128)(2,1)}), bf16[64,1,4,768]{3,2,1,0:T(4,128)(2,1)S(1)}, u32[]{:S(2)}, u32[]{:S(2)}) async-start(bf16[64,1,4,768]{3,2,1,0:T(4,128)(2,1)} %reshape.152), calls=%async_computation.2 | async-start | bytes 786432 | tf_op jit(solution)/shard_map/all_to_all | solution.py:33
  247.7 16.3 %copy-start.5 = (bf16[64,1,4,768]{3,2,1,0:T(4,128)(2,1)}, bf16[64,1,4,768]{3,2,1,0:T(4,128)(2,1)S(1)}, u32[]{:S(2)}) copy-start(bf16[64,1,4,768]{3,2,1,0:T(4,128)(2,1)S(1)} %all-to-all-done.2) | copy-start | bytes 1179652
  247.7 27.0 %all-to-all-start.3 = ((bf16[64,1,4,768]{3,2,1,0:T(4,128)(2,1)}), bf16[64,1,4,768]{3,2,1,0:T(4,128)(2,1)}, u32[]{:S(2)}, u32[]{:S(2)}) async-start(bf16[64,1,4,768]{3,2,1,0:T(4,128)(2,1)} %reshape.154), calls=%async_computation.3 | async-start | bytes 786432 | tf_op jit(solution)/shard_map/all_to_all | solution.py:33
  258.9 275.0 %all-reduce.2.cloned.1.call-start = ((), (), s32[]{:S(2)}) async-start(), calls=%async_computation.8 | async-start | bytes 1572864 | tf_op jit(solution)/shard_map/psum | solution.py:100
  259.2 4.9 copy-start.3
  259.2 4.9 copy-start.9
  264.1 4.0 copy-start.1
  268.4 9.7 %copy-start.6 = (f32[196,256]{1,0:T(8,128)}, f32[196,256]{1,0:T(8,128)S(1)}, u32[]{:S(2)}) copy-start(f32[196,256]{1,0:T(8,128)S(1)} %convolution_bitcast_fusion.1) | copy-start | bytes 602116
Sparse Core Ops, SparseCore 0:
  53.0 48.9 all-gather.4
  103.8 41.0 all-gather.2
  155.1 39.9 reduce-scatter.8
  197.5 48.1 reduce-scatter.10
  280.5 253.3 all-reduce.1
where the time goes:
time: 543 us; the launch traced here: 542 us
  waiting for transfers between devices  374 us (69%)
  blocking collectives  55.4 us (10%)
  local copies, waits for them, and re-layouts  37.9 us (7%)
  matrix products  29 us (5%)
  starting transfers between devices  22.8 us (4%)
  between operations  14 us (3%)
  other arithmetic  8.99 us (2%)
    psum x1, waiting for transfers between devices, per_device(): router_sum = lax.psum(router_term, ('expert', 'hidden'))  251 us
    unnamed x7, waiting for transfers between devices  71.7 us
    all_to_all x2, blocking collectives, to_experts(): lax.all_to_all(stacked_slots, 'expert', split_axis=2, concat_axis=0, tile...  55.4 us
    all_gather x2, waiting for transfers between devices, to_experts(): arrived = lax.all_gather(crossed, 'hidden', axis=0, tiled=True)  44.3 us
    all_to_all x2, starting transfers between devices, to_owners(): lax.all_to_all(summed, 'expert', split_axis=0, concat_axis=2, tiled=True)  22 us
    unnamed x29, local copies, waits for them, and re-layouts  15.3 us
  transfers between devices with their start and end apart: 7, of which 6 were waited for; matrix products, arithmetic and copies ran while one was open for 7% of the time, Pallas kernels for 0%

commit v1 on v0

--- a/solution.py
+++ b/solution.py
@@ -20,7 +20,12 @@
 
 
 def to_experts(stacked_slots):
-    crossed = lax.all_to_all(stacked_slots, "expert", split_axis=2, concat_axis=0, tiled=True)
+    crossed = jnp.concatenate(
+        lax.all_to_all(
+            jnp.stack(jnp.split(stacked_slots, lax.axis_size("expert"), axis=2)), "expert", 0, 0
+        ),
+        axis=0,
+    )
     arrived = lax.all_gather(crossed, "hidden", axis=0, tiled=True)
     return arrived
 

time: 543 us -> 568 us (1.046)
  blocking collectives: 55.4 us -> 26.2 us
  local copies, waits for them, and re-layouts: 37.9 us -> 64.3 us
  waiting for transfers between devices: 374 us -> 396 us
  starting transfers between devices: 22.8 us -> 37 us
  other arithmetic: 8.99 us -> 1.29 us
    unnamed x29 -> x154, local copies, waits for them, and re-layouts: 15.3 us -> 51.1 us
    all_to_all x2 -> x1, blocking collectives: 55.4 us -> 26.2 us  [to_experts(): lax.all_to_all(jnp.stack(jnp.split(stacked_slots, lax.axis_size('expert')...]
    all_to_all x0 -> x1, starting transfers between devices: none -> 14.6 us  [to_experts(): lax.all_to_all(jnp.stack(jnp.split(stacked_slots, lax.axis_size('expert')...]
    all_to_all x0 -> x1, waiting for transfers between devices: none -> 12.7 us  [to_experts(): lax.all_to_all(jnp.stack(jnp.split(stacked_slots, lax.axis_size('expert')...]
    all_gather x2, waiting for transfers between devices: 44.3 us -> 55.2 us  [to_experts(): arrived = lax.all_gather(crossed, 'hidden', axis=0, tiled=True)]
    all_to_all x4 -> x0, local copies, waits for them, and re-layouts: 9.7 us -> none  [to_experts(): lax.all_to_all(stacked_slots, 'expert', split_axis=2, concat_axis=0, tile...]
    unnamed x2 -> x0, other arithmetic: 7.7 us -> none
  transfers between devices with their start and end apart: 7 -> 8, of which waited for: 6 -> 7; matrix products, arithmetic and copies ran while one was open for 7% -> 6% of each run, Pallas kernels for 0% -> 0%
where the time goes in v1:
time: 568 us; the launch traced here: 567 us
  waiting for transfers between devices  396 us (70%)
  local copies, waits for them, and re-layouts  64.3 us (11%)
  starting transfers between devices  37 us (7%)
  matrix products  28 us (5%)
  blocking collectives  26.2 us (5%)
  between operations  14.3 us (3%)
    psum x1, waiting for transfers between devices, per_device(): router_sum = lax.psum(router_term, ('expert', 'hidden'))  251 us
    unnamed x7, waiting for transfers between devices  71.5 us
    all_gather x2, waiting for transfers between devices, to_experts(): arrived = lax.all_gather(crossed, 'hidden', axis=0, tiled=True)  55.2 us
    unnamed x154, local copies, waits for them, and re-layouts  51.1 us
    all_to_all x1, blocking collectives, to_experts(): lax.all_to_all(jnp.stack(jnp.split(stacked_slots, lax.axis_size('expert')...  26.2 us
    all_to_all x2, starting transfers between devices, to_owners(): lax.all_to_all(summed, 'expert', split_axis=0, concat_axis=2, tiled=True)  22 us
    all_to_all x1, starting transfers between devices, to_experts(): lax.all_to_all(jnp.stack(jnp.split(stacked_slots, lax.axis_size('expert')...  14.6 us
    all_to_all x1, waiting for transfers between devices, to_experts(): lax.all_to_all(jnp.stack(jnp.split(stacked_slots, lax.axis_size('expert')...  12.7 us
  transfers between devices with their start and end apart: 8, of which 7 were waited for; matrix products, arithmetic and copies ran while one was open for 6% of the time, Pallas kernels for 0%

profile of v1, /device:TPU:2, one launch (start us, length us, event | category | flops | bytes accessed | tf_op | source)
XLA Modules:
  0.0 567.2 jit_solution(12447457285687064407)
XLA Ops:
  7.2 1.6 fusion.40
  9.0 1.3 fusion.28
  48.6 14.6 %all-to-all-start.1 = ((bf16[64,1,1,4,768]{4,3,2,1,0:T(4,128)(2,1)}), bf16[64,1,1,4,768]{4,3,2,1,0:T(4,128)(2,1)S(1)}, u32[]{:S(2)}, u32[]{:S(2)}) async-start(bf16[64,1,1,4,768]{4,3,2,1,0:T(4,128)(2,1)} %constant_dynamic-update-slice_fusion.64), calls=%async_computation.1 | async-start | bytes 786432 | tf_op jit(solution)/shard_map/all_to_all | solution.py:24
  64.7 12.7 %all-to-all-done.1 = bf16[64,1,1,4,768]{4,3,2,1,0:T(4,128)(2,1)S(1)} async-done(((bf16[64,1,1,4,768]{4,3,2,1,0:T(4,128)(2,1)}), bf16[64,1,1,4,768]{4,3,2,1,0:T(4,128)(2,1)S(1)}, u32[]{:S(2)}, u32[]{:S(2)}) %all-to-all-start.1) | async-done | bytes 393248 | tf_op jit(solution)/shard_map/all_to_all | solution.py:24
  84.0 26.2 %all_to_all.28 = bf16[64,1,1,4,768]{4,3,2,1,0:T(4,128)(2,1)} all-to-all(bf16[64,1,1,4,768]{4,3,2,1,0:T(4,128)(2,1)S(1)} %constant_dynamic-update-slice_fusion), channel_id=1, replica_groups=mesh['expert'=64,'hidden'=4] {'expert'}, dimensions={0} | all-to-all | bytes 786432 | tf_op jit(solution)/shard_map/all_to_all | solution.py:24
  110.3 16.4 %all-gather.7.cloned.1.call-done = bf16[256,1,1,4,768]{4,3,2,1,0:T(4,128)(2,1)} async-done(((bf16[64,1,1,4,768]{4,3,2,1,0:T(4,128)(2,1)}), bf16[256,1,1,4,768]{4,3,2,1,0:T(4,128)(2,1)}) %all-gather.7.cloned.1.call-update) | async-done | bytes 1572880 | tf_op jit(solution)/shard_map/all_gather | solution.py:29
  126.7 1.6 copy.22
  128.3 3.1 fusion.9
  131.4 38.8 %all-gather.5.cloned.1.call-done = bf16[256,1,1,4,768]{4,3,2,1,0:T(4,128)(2,1)} async-done(((bf16[64,1,1,4,768]{4,3,2,1,0:T(4,128)(2,1)}), bf16[256,1,1,4,768]{4,3,2,1,0:T(4,128)(2,1)}) %all-gather.5.cloned.1.call-update) | async-done | bytes 1572880 | tf_op jit(solution)/shard_map/all_gather | solution.py:29
  170.2 1.8 copy.21
  172.4 3.8 fusion.5
  176.1 1.4 fusion.21
  177.6 1.2 copy.37
  178.8 1.4 copy.43
  180.5 3.5 fusion.18
  184.0 1.2 copy.39
  185.3 1.4 copy.44
  186.7 33.7 %reduce-scatter.9.cloned.1.call-done = bf16[64,3072]{1,0:T(8,128)(2,1)} async-done(((bf16[256,3072]{1,0:T(8,128)(2,1)}), bf16[64,3072]{1,0:T(8,128)(2,1)}) %reduce-scatter.9.cloned.1.call-update) | async-done | bytes 393232
  220.4 2.0 reshape.158
  222.4 10.8 %all-to-all-start.2 = ((bf16[64,1,4,768]{3,2,1,0:T(4,128)(2,1)}), bf16[64,1,4,768]{3,2,1,0:T(4,128)(2,1)S(1)}, u32[]{:S(2)}, u32[]{:S(2)}) async-start(bf16[64,1,4,768]{3,2,1,0:T(4,128)(2,1)} %reshape.158), calls=%async_computation.2 | async-start | bytes 786432 | tf_op jit(solution)/shard_map/all_to_all | solution.py:38
  233.3 37.7 %reduce-scatter.11.cloned.1.call-done = bf16[64,3072]{1,0:T(8,128)(2,1)} async-done(((bf16[256,3072]{1,0:T(8,128)(2,1)}), bf16[64,3072]{1,0:T(8,128)(2,1)}) %reduce-scatter.11.cloned.1.call-update) | async-done | bytes 393232
  271.0 2.0 reshape.160
  273.0 11.1 %all-to-all-start.3 = ((bf16[64,1,4,768]{3,2,1,0:T(4,128)(2,1)}), bf16[64,1,4,768]{3,2,1,0:T(4,128)(2,1)}, u32[]{:S(2)}, u32[]{:S(2)}) async-start(bf16[64,1,4,768]{3,2,1,0:T(4,128)(2,1)} %reshape.160), calls=%async_computation.3 | async-start | bytes 786432 | tf_op jit(solution)/shard_map/all_to_all | solution.py:38
  284.2 4.8 bitcast_convert_fusion
  290.5 2.9 bitcast_convert_fusion.1
  294.8 5.3 all-to-all-done.3
  300.1 1.8 reshape.148
  301.9 1.5 multiply_reduce_fusion.1
  304.5 1.2 convolution_bitcast_fusion
  306.0 2.0 fusion.26
  308.0 251.3 %all-reduce.2.cloned.1.call-done = f32[768,256]{0,1:T(8,128)} async-done(((f32[768,256]{0,1:T(8,128)}), f32[768,256]{0,1:T(8,128)}) %all-reduce.2.cloned.1.call-update) | async-done | bytes 786448 | tf_op jit(solution)/shard_map/psum | solution.py:105
  559.3 1.4 dynamic_slice.3
  (170 shorter events, 51.1 us)
Async XLA Ops:
  7.2 121.1 %copy-start = (bf16[2,768,768]{2,1,0:T(8,128)(2,1)S(1)}, bf16[2,768,768]{2,1,0:T(8,128)(2,1)}, u32[]{:S(2)}) copy-start(bf16[2,768,768]{2,1,0:T(8,128)(2,1)} %param.8) | copy-start | bytes 7077892
  7.2 56.1 %copy-start.9 = (bf16[196,768]{1,0:T(8,128)(2,1)S(1)}, bf16[196,768]{1,0:T(8,128)(2,1)}, u32[]{:S(2)}) copy-start(bf16[196,768]{1,0:T(8,128)(2,1)} %param.6) | copy-start | bytes 903172
  48.6 28.8 %all-to-all-start.1 = ((bf16[64,1,1,4,768]{4,3,2,1,0:T(4,128)(2,1)}), bf16[64,1,1,4,768]{4,3,2,1,0:T(4,128)(2,1)S(1)}, u32[]{:S(2)}, u32[]{:S(2)}) async-start(bf16[64,1,1,4,768]{4,3,2,1,0:T(4,128)(2,1)} %constant_dynamic-update-slice_fusion.64), calls=%async_computation.1 | async-start | bytes 786432 | tf_op jit(solution)/shard_map/all_to_all | solution.py:24
  63.2 63.5 %all-gather.7.cloned.1.call-start = ((), (), s32[]{:S(2)}) async-start(), calls=%async_computation.8 | async-start | bytes 1966080 | tf_op jit(solution)/shard_map/all_gather | solution.py:29
  63.7 0.9 copy-start.7
  77.4 0.7 copy-start.4
  78.2 92.0 %all-gather.5.cloned.1.call-start = ((), (), s32[]{:S(2)}) async-start(), calls=%async_computation.7 | async-start | bytes 1966080 | tf_op jit(solution)/shard_map/all_gather | solution.py:29
  110.3 110.2 %reduce-scatter.9.cloned.1.call-start = ((), (), s32[]{:S(2)}) async-start(), calls=%async_computation.9 | async-start | bytes 1966080
  170.2 2.1 copy-start.8
  172.0 4.1 copy-start.3
  176.1 1.4 copy-start.10
  180.3 90.7 %reduce-scatter.11.cloned.1.call-start = ((), (), s32[]{:S(2)}) async-start(), calls=%async_computation.10 | async-start | bytes 1966080
  222.4 50.6 %all-to-all-start.2 = ((bf16[64,1,4,768]{3,2,1,0:T(4,128)(2,1)}), bf16[64,1,4,768]{3,2,1,0:T(4,128)(2,1)S(1)}, u32[]{:S(2)}, u32[]{:S(2)}) async-start(bf16[64,1,4,768]{3,2,1,0:T(4,128)(2,1)} %reshape.158), calls=%async_computation.2 | async-start | bytes 786432 | tf_op jit(solution)/shard_map/all_to_all | solution.py:38
  273.0 16.0 %copy-start.5 = (bf16[64,1,4,768]{3,2,1,0:T(4,128)(2,1)}, bf16[64,1,4,768]{3,2,1,0:T(4,128)(2,1)S(1)}, u32[]{:S(2)}) copy-start(bf16[64,1,4,768]{3,2,1,0:T(4,128)(2,1)S(1)} %all-to-all-done.2) | copy-start | bytes 1179652
  273.0 27.1 %all-to-all-start.3 = ((bf16[64,1,4,768]{3,2,1,0:T(4,128)(2,1)}), bf16[64,1,4,768]{3,2,1,0:T(4,128)(2,1)}, u32[]{:S(2)}, u32[]{:S(2)}) async-start(bf16[64,1,4,768]{3,2,1,0:T(4,128)(2,1)} %reshape.160), calls=%async_computation.3 | async-start | bytes 786432 | tf_op jit(solution)/shard_map/all_to_all | solution.py:38
  284.2 275.1 %all-reduce.2.cloned.1.call-start = ((), (), s32[]{:S(2)}) async-start(), calls=%async_computation.6 | async-start | bytes 1572864 | tf_op jit(solution)/shard_map/psum | solution.py:105
  284.2 4.9 copy-start.1
  289.1 1.4 copy-start.11
  290.5 4.0 copy-start.2
  294.8 8.7 %copy-start.6 = (f32[196,256]{1,0:T(8,128)}, f32[196,256]{1,0:T(8,128)S(1)}, u32[]{:S(2)}) copy-start(f32[196,256]{1,0:T(8,128)S(1)} %convolution_bitcast_fusion.1) | copy-start | bytes 602116
Sparse Core Ops, SparseCore 0:
  78.3 48.3 all-gather.6
  128.5 41.6 all-gather.4
  180.4 39.9 reduce-scatter.8
  222.8 48.1 reduce-scatter.10
  305.9 253.3 all-reduce.1
